TPU v7x, 256 devices: a whole 4x4x8 slice. The times are simulated.
256 devices in a mesh: row: 8 (over z), col: 32 (over x, y, core).
Axes of the slice: x: 4, y: 4, z: 8, core: 2. Of those that a mesh axis runs over, the one named last changes fastest.
Arguments:
- inputs: bfloat16 [1024, 16, 1024], P('col', 'row'), may hold values from -6 to 6
- weight: bfloat16 [1024, 27, 1024], P('col', None, 'row'), may hold values from -0.0390625 to 0.0390625
- grad_out: bfloat16 [1024, 16, 1024], P('col', 'row'), may hold values from -6 to 6
Outputs:
- outputs: bfloat16 [1024, 16, 1024], P('col', 'row')
- grad_in: bfloat16 [1024, 16, 1024], P('col', 'row')
- grad_weight: float32 [1024, 27, 1024], P('col', None, 'row')
All inputs are finite; a program needn't handle non-finite values.
Results may differ from a plain program's by a relative error of at most 0.0011.
Values may be sent and summed in bfloat16 or wider, within the bound.
A program may use at most 128 MiB of HBM per device.

v0:
```python
import math
import jax
import jax.numpy as jnp
from jax import lax
from jax.sharding import PartitionSpec as P

BX = 32
BY = 32
kernel_offsets = [(a, b, e) for a in (-1, 0, 1) for b in (-1, 0, 1) for e in (-1, 0, 1)]


def extended(block, sides, width):
    for axis, dim in sides:
        count = lax.axis_size(axis)
        forward = [(i, i + 1) for i in range(count - 1)]
        backward = [(target, source) for source, target in forward]
        low = lax.ppermute(
            lax.slice_in_dim(block, block.shape[dim] - width, None, axis=dim), axis, forward
        )
        high = lax.ppermute(lax.slice_in_dim(block, 0, width, axis=dim), axis, backward)
        block = jnp.concatenate([low, block, high], axis=dim)
    return block


def plane_valid(shift_y, shift_x, extent):
    positions = jnp.arange(extent, dtype=jnp.int32) % (BY * BX)
    along_y = positions // BX + shift_y
    along_x = positions % BX + shift_x
    return (along_y >= 0) & (along_y < BY) & (along_x >= 0) & (along_x < BX)


def flat_rim(field):
    flattened = field.reshape(field.shape[0], -1)
    return jnp.pad(flattened, ((0, 0), (BX + 1, BX + 1)))


def shifted(flattened, planes, shift_z, shift_y, shift_x):
    extent = planes * BY * BX
    offset = BX + 1 + (1 + shift_z) * BY * BX + shift_y * BX + shift_x
    window = lax.slice_in_dim(flattened, offset, offset + extent, axis=1)
    return jnp.where(plane_valid(shift_y, shift_x, extent)[None, :], window, jnp.zeros_like(window))


def forward_columns(padded, planes):
    windows = [shifted(padded, planes, sz, sy, sx) for sz, sy, sx in kernel_offsets]
    stacked = jnp.stack(windows, axis=0)
    return stacked.reshape(27 * padded.shape[0], stacked.shape[2])


def backward_columns(padded, planes):
    windows = [shifted(padded, planes, -sz, -sy, -sx) for sz, sy, sx in kernel_offsets]
    stacked = jnp.stack(windows, axis=1)
    return stacked.reshape(padded.shape[0] * 27, stacked.shape[2])


def group_count(shard_count, unit):
    target = max(1, 128 // unit)
    best = 1
    for candidate in range(1, shard_count + 1):
        if shard_count % candidate == 0 and candidate <= target:
            best = candidate
    return best


def on_device(inputs, weight, grad_out):
    width_dev = inputs.shape[0]
    planes = inputs.shape[1]
    extent = planes * BY * BX
    gathered_weight = lax.all_gather(weight, "row", axis=2, tiled=True)
    out_width = gathered_weight.shape[0]
    channels = gathered_weight.shape[2]
    input_rim = extended(inputs, (("row", 1),), 1)
    grad_rim = extended(grad_out, (("row", 1),), 1)
    grad_rows = grad_out.reshape(out_width, extent)
    initial = (
        jnp.zeros((out_width, extent), jnp.float32),
        jnp.zeros((channels, 27 * out_width), jnp.float32),
    )
    shard_rows = lax.all_gather(input_rim, "col", axis=0, tiled=True)
    shard_count = shard_rows.shape[0] // width_dev
    group = group_count(shard_count, width_dev)
    block_rows = group * width_dev
    count_blocks = shard_count // group

    def one_block(b, state):
        output_sum, weight_sum = state
        first_channel = b * block_rows
        channel_block = lax.dynamic_slice_in_dim(shard_rows, b * block_rows, block_rows, 0)
        columns = forward_columns(flat_rim(channel_block), planes)
        weight_block = lax.dynamic_slice_in_dim(gathered_weight, first_channel, block_rows, 2)
        flat_weight = weight_block.reshape(out_width, 27 * block_rows)
        output_sum = output_sum + jnp.dot(flat_weight, columns, preferred_element_type=jnp.float32)
        block_grad = lax.dot_general(
            columns, grad_rows, (((1,), (1,)), ((), ())), preferred_element_type=jnp.float32
        )
        block_grad = block_grad.reshape(27, block_rows, out_width).transpose(1, 0, 2)
        block_grad = block_grad.reshape(block_rows, 27 * out_width)
        weight_sum = lax.dynamic_update_slice_in_dim(weight_sum, block_grad, first_channel, 0)
        return (output_sum, weight_sum)

    output_sum, weight_rows_sum = lax.fori_loop(0, count_blocks, one_block, initial)
    outputs = output_sum.astype(jnp.bfloat16).reshape(out_width, planes, BY * BX)
    weight_sum = weight_rows_sum.reshape(channels, 27, out_width).transpose(2, 1, 0)
    scale = 1.0 / math.sqrt(planes * lax.axis_size("row") * BY * BX)
    grad_weight = lax.psum_scatter(weight_sum, "row", scatter_dimension=2, tiled=True) * scale
    grad_columns = backward_columns(flat_rim(grad_rim), planes)
    flat_cols = gathered_weight.reshape(out_width * 27, width_dev * lax.axis_size("col"))
    grad_sum = lax.psum_scatter(
        lax.dot_general(
            flat_cols, grad_columns, (((0,), (0,)), ((), ())), preferred_element_type=jnp.float32
        ),
        "col",
        scatter_dimension=0,
        tiled=True,
    )
    grad_in = grad_sum.astype(jnp.bfloat16).reshape(width_dev, planes, BY * BX)
    return (outputs, grad_in, grad_weight)


def solution(mesh):
    placed = (P("col", "row", None), P("col", None, "row"), P("col", "row", None))
    return jax.shard_map(
        on_device,
        mesh=mesh,
        in_specs=placed,
        out_specs=(P("col", "row", None), P("col", "row", None), P("col", None, "row")),
        check_vma=False,
    )
```

profile of v0, /device:TPU:1, one launch (start us, length us, event | category | flops | bytes accessed | tf_op | source)
XLA Modules:
  0.0 399.2 jit_solution(570935348018330792)
XLA Ops:
  7.2 0.7 all-gather.3.cloned.1.call-update
  7.9 1.2 fusion.94
  9.2 1.3 collective-permute-start.1
  10.5 5.0 %collective-permute-start = (bf16[32,1,1024]{2,1,0:T(2,128)(2,1)S(1)}, bf16[32,1,1024]{2,1,0:T(2,128)(2,1)S(1)}, u32[]{:S(2)}, u32[]{:S(2)}) collective-permute-start(bf16[32,1,1024]{2,1,0:T(2,128)(2,1)S(1)} %get-tuple-element.234), channel_id=1, source_target_pairs={{0,32},{32,64},{64,96},{96,128},{128,160},{160,192},{192,224},{1,3... | collective-permute-start | bytes 196616 | tf_op jit(solution)/shard_map/ppermute | solution.py:17
  15.9 1.5 collective-permute-done
  17.4 2.1 pad_maximum_fusion
  19.5 1.2 fusion.93
  20.8 1.3 collective-permute-start.3
  22.1 4.4 %collective-permute-start.2 = (bf16[32,1,1024]{2,1,0:T(2,128)(2,1)S(1)}, bf16[32,1,1024]{2,1,0:T(2,128)(2,1)S(1)}, u32[]{:S(2)}, u32[]{:S(2)}) collective-permute-start(bf16[32,1,1024]{2,1,0:T(2,128)(2,1)S(1)} %get-tuple-element.232), channel_id=1, source_target_pairs={{0,32},{32,64},{64,96},{96,128},{128,160},{160,192},{192,224},{1,3... | collective-permute-start | bytes 196616 | tf_op jit(solution)/shard_map/ppermute | solution.py:17
  26.5 1.6 copy.11
  28.5 1.3 pad_maximum_fusion.1
  32.7 23.8 %all-gather.3.cloned.1.call-done = bf16[32,27,1024]{2,0,1:T(8,128)(2,1)} async-done(((bf16[32,27,128]{2,0,1:T(8,128)(2,1)}), bf16[32,27,1024]{2,0,1:T(8,128)(2,1)}) %all-gather.3.cloned.1.call-update) | async-done | bytes 1769488 | tf_op jit(solution)/shard_map/all_gather | solution.py:69
  56.5 8.2 %convolution_bitcast_fusion.1 = f32[1024,2048]{0,1:T(8,128)} fusion(bf16[32,27,2048]{2,0,1:T(8,128)(2,1)S(1)} %bitcast_dynamic-update-slice_fusion.8, bf16[32,27,1024]{2,0,1:T(8,128)(2,1)} %all-gather.3.cloned.1.call-done), kind=kOutput, calls=%fused_computation.105 | convolution fusion | flops 3623878656 | bytes 13697024 | tf_op jit(solution)/shard_map/dot_general | solution.py:109
  64.7 9.1 %copy.8 = f32[1024,2048]{1,0:T(8,128)} copy(f32[1024,2048]{0,1:T(8,128)} %convolution_bitcast_fusion.1) | data formatting | bytes 16777216
  73.9 46.7 %all-gather.5.cloned.1.call-done = bf16[1024,4,1024]{2,1,0:T(4,128)(2,1)} async-done(((bf16[32,4,1024]{2,1,0:T(4,128)(2,1)}), bf16[1024,4,1024]{2,1,0:T(4,128)(2,1)}) %all-gather.5.cloned.1.call-update) | async-done | bytes 8388624 | tf_op jit(solution)/shard_map/all_gather | solution.py:79
  120.6 0.4 broadcast_in_dim.490
  121.0 219.4 %while.19 = (s32[]{:T(128)}, f32[32,2048]{1,0:T(8,128)}, f32[1024,864]{0,1:T(8,128)S(1)}, bf16[32,27,1024]{2,0,1:T(8,128)(2,1)}, bf16[1024,4,1024]{2,1,0:T(4,128...) while((s32[]{:T(128)}, f32[32,2048]{1,0:T(8,128)}, ...), condition=%wide.region_1.2_spmd.clone, body=%wide.region_0.1_spmd.clone.sunk | while | flops 913793024 | bytes 181059872 | solution.py:101
  121.2 1.6 constant_dynamic-slice_fusion.2
  129.5 5.0 %copy-done = bf16[27,128,2048]{2,1,0:T(8,128)(2,1)} copy-done((bf16[27,128,2048]{2,1,0:T(8,128)(2,1)}, bf16[27,128,2048]{2,1,0:T(8,128)(2,1)S(1)}, u32[]{:S(2)}) %copy-start) | copy-done | bytes 14155800 | tf_op jit(solution)/shard_map/while
  134.5 9.1 %fusion.147 = f32[32,2048]{1,0:T(8,128)} fusion(bf16[27,128,2048]{2,1,0:T(8,128)(2,1)} %copy-done, f32[32,2048]{1,0:T(8,128)} %get-tuple-element.284, bf16[32,27,1024]{2,0,1:T(8,128)(2,1)} %get-tuple-element.296, s32[]{:T(128)S(6)} %select_n.2038, pred[]{:T(512)S(6)} %compare.180), kind=kOutput, calls=%fused_computation.1.clone.1 | convolution fusion | flops 453115904 | bytes 14901253 | tf_op jit(solution)/shard_map/while/body/eval_jaxpr/dot_general | solution.py:92
  143.6 1.4 copy-done.1
  145.0 4.3 %fusion.148 = f32[27,128,32]{1,2,0:T(8,128)S(1)} fusion(bf16[27,128,2048]{2,1,0:T(8,128)(2,1)S(1)} %copy-done.1, bf16[32,2048]{1,0:T(8,128)(2,1)S(1)} %copy-done.3), kind=kOutput, calls=%fused_computation.68.clone.1 | convolution fusion | flops 452984832 | bytes 14729216 | tf_op jit(solution)/shard_map/while/body/eval_jaxpr/dot_general | solution.py:93
  149.4 1.7 constant_dynamic-slice_fusion.2
  157.7 5.5 %copy-done = bf16[27,128,2048]{2,1,0:T(8,128)(2,1)} copy-done((bf16[27,128,2048]{2,1,0:T(8,128)(2,1)}, bf16[27,128,2048]{2,1,0:T(8,128)(2,1)S(1)}, u32[]{:S(2)}) %copy-start) | copy-done | bytes 14155800 | tf_op jit(solution)/shard_map/while
  163.2 8.8 %fusion.147 = f32[32,2048]{1,0:T(8,128)} fusion(bf16[27,128,2048]{2,1,0:T(8,128)(2,1)} %copy-done, f32[32,2048]{1,0:T(8,128)} %get-tuple-element.284, bf16[32,27,1024]{2,0,1:T(8,128)(2,1)} %get-tuple-element.296, s32[]{:T(128)S(6)} %select_n.2038, pred[]{:T(512)S(6)} %compare.180), kind=kOutput, calls=%fused_computation.1.clone.1 | convolution fusion | flops 453115904 | bytes 14901253 | tf_op jit(solution)/shard_map/while/body/eval_jaxpr/dot_general | solution.py:92
  172.1 0.8 copy-done.1
  172.9 4.3 %fusion.148 = f32[27,128,32]{1,2,0:T(8,128)S(1)} fusion(bf16[27,128,2048]{2,1,0:T(8,128)(2,1)S(1)} %copy-done.1, bf16[32,2048]{1,0:T(8,128)(2,1)S(1)} %copy-done.3), kind=kOutput, calls=%fused_computation.68.clone.1 | convolution fusion | flops 452984832 | bytes 14729216 | tf_op jit(solution)/shard_map/while/body/eval_jaxpr/dot_general | solution.py:93
  177.3 1.6 constant_dynamic-slice_fusion.2
  185.6 5.1 %copy-done = bf16[27,128,2048]{2,1,0:T(8,128)(2,1)} copy-done((bf16[27,128,2048]{2,1,0:T(8,128)(2,1)}, bf16[27,128,2048]{2,1,0:T(8,128)(2,1)S(1)}, u32[]{:S(2)}) %copy-start) | copy-done | bytes 14155800 | tf_op jit(solution)/shard_map/while
  190.7 8.7 %fusion.147 = f32[32,2048]{1,0:T(8,128)} fusion(bf16[27,128,2048]{2,1,0:T(8,128)(2,1)} %copy-done, f32[32,2048]{1,0:T(8,128)} %get-tuple-element.284, bf16[32,27,1024]{2,0,1:T(8,128)(2,1)} %get-tuple-element.296, s32[]{:T(128)S(6)} %select_n.2038, pred[]{:T(512)S(6)} %compare.180), kind=kOutput, calls=%fused_computation.1.clone.1 | convolution fusion | flops 453115904 | bytes 14901253 | tf_op jit(solution)/shard_map/while/body/eval_jaxpr/dot_general | solution.py:92
  199.4 1.1 copy-done.1
  200.5 4.3 %fusion.148 = f32[27,128,32]{1,2,0:T(8,128)S(1)} fusion(bf16[27,128,2048]{2,1,0:T(8,128)(2,1)S(1)} %copy-done.1, bf16[32,2048]{1,0:T(8,128)(2,1)S(1)} %copy-done.3), kind=kOutput, calls=%fused_computation.68.clone.1 | convolution fusion | flops 452984832 | bytes 14729216 | tf_op jit(solution)/shard_map/while/body/eval_jaxpr/dot_general | solution.py:93
  204.9 1.6 constant_dynamic-slice_fusion.2
  213.2 5.0 %copy-done = bf16[27,128,2048]{2,1,0:T(8,128)(2,1)} copy-done((bf16[27,128,2048]{2,1,0:T(8,128)(2,1)}, bf16[27,128,2048]{2,1,0:T(8,128)(2,1)S(1)}, u32[]{:S(2)}) %copy-start) | copy-done | bytes 14155800 | tf_op jit(solution)/shard_map/while
  218.2 8.7 %fusion.147 = f32[32,2048]{1,0:T(8,128)} fusion(bf16[27,128,2048]{2,1,0:T(8,128)(2,1)} %copy-done, f32[32,2048]{1,0:T(8,128)} %get-tuple-element.284, bf16[32,27,1024]{2,0,1:T(8,128)(2,1)} %get-tuple-element.296, s32[]{:T(128)S(6)} %select_n.2038, pred[]{:T(512)S(6)} %compare.180), kind=kOutput, calls=%fused_computation.1.clone.1 | convolution fusion | flops 453115904 | bytes 14901253 | tf_op jit(solution)/shard_map/while/body/eval_jaxpr/dot_general | solution.py:92
  226.9 0.8 copy-done.1
  227.7 4.3 %fusion.148 = f32[27,128,32]{1,2,0:T(8,128)S(1)} fusion(bf16[27,128,2048]{2,1,0:T(8,128)(2,1)S(1)} %copy-done.1, bf16[32,2048]{1,0:T(8,128)(2,1)S(1)} %copy-done.3), kind=kOutput, calls=%fused_computation.68.clone.1 | convolution fusion | flops 452984832 | bytes 14729216 | tf_op jit(solution)/shard_map/while/body/eval_jaxpr/dot_general | solution.py:93
  232.2 1.6 constant_dynamic-slice_fusion.2
  240.4 5.0 %copy-done = bf16[27,128,2048]{2,1,0:T(8,128)(2,1)} copy-done((bf16[27,128,2048]{2,1,0:T(8,128)(2,1)}, bf16[27,128,2048]{2,1,0:T(8,128)(2,1)S(1)}, u32[]{:S(2)}) %copy-start) | copy-done | bytes 14155800 | tf_op jit(solution)/shard_map/while
  245.5 8.5 %fusion.147 = f32[32,2048]{1,0:T(8,128)} fusion(bf16[27,128,2048]{2,1,0:T(8,128)(2,1)} %copy-done, f32[32,2048]{1,0:T(8,128)} %get-tuple-element.284, bf16[32,27,1024]{2,0,1:T(8,128)(2,1)} %get-tuple-element.296, s32[]{:T(128)S(6)} %select_n.2038, pred[]{:T(512)S(6)} %compare.180), kind=kOutput, calls=%fused_computation.1.clone.1 | convolution fusion | flops 453115904 | bytes 14901253 | tf_op jit(solution)/shard_map/while/body/eval_jaxpr/dot_general | solution.py:92
  254.0 0.8 copy-done.1
  254.8 4.3 %fusion.148 = f32[27,128,32]{1,2,0:T(8,128)S(1)} fusion(bf16[27,128,2048]{2,1,0:T(8,128)(2,1)S(1)} %copy-done.1, bf16[32,2048]{1,0:T(8,128)(2,1)S(1)} %copy-done.3), kind=kOutput, calls=%fused_computation.68.clone.1 | convolution fusion | flops 452984832 | bytes 14729216 | tf_op jit(solution)/shard_map/while/body/eval_jaxpr/dot_general | solution.py:93
  259.2 1.6 constant_dynamic-slice_fusion.2
  267.5 5.0 %copy-done = bf16[27,128,2048]{2,1,0:T(8,128)(2,1)} copy-done((bf16[27,128,2048]{2,1,0:T(8,128)(2,1)}, bf16[27,128,2048]{2,1,0:T(8,128)(2,1)S(1)}, u32[]{:S(2)}) %copy-start) | copy-done | bytes 14155800 | tf_op jit(solution)/shard_map/while
  272.5 8.5 %fusion.147 = f32[32,2048]{1,0:T(8,128)} fusion(bf16[27,128,2048]{2,1,0:T(8,128)(2,1)} %copy-done, f32[32,2048]{1,0:T(8,128)} %get-tuple-element.284, bf16[32,27,1024]{2,0,1:T(8,128)(2,1)} %get-tuple-element.296, s32[]{:T(128)S(6)} %select_n.2038, pred[]{:T(512)S(6)} %compare.180), kind=kOutput, calls=%fused_computation.1.clone.1 | convolution fusion | flops 453115904 | bytes 14901253 | tf_op jit(solution)/shard_map/while/body/eval_jaxpr/dot_general | solution.py:92
  281.1 0.8 copy-done.1
  281.9 4.3 %fusion.148 = f32[27,128,32]{1,2,0:T(8,128)S(1)} fusion(bf16[27,128,2048]{2,1,0:T(8,128)(2,1)S(1)} %copy-done.1, bf16[32,2048]{1,0:T(8,128)(2,1)S(1)} %copy-done.3), kind=kOutput, calls=%fused_computation.68.clone.1 | convolution fusion | flops 452984832 | bytes 14729216 | tf_op jit(solution)/shard_map/while/body/eval_jaxpr/dot_general | solution.py:93
  286.3 1.6 constant_dynamic-slice_fusion.2
  294.5 5.0 %copy-done = bf16[27,128,2048]{2,1,0:T(8,128)(2,1)} copy-done((bf16[27,128,2048]{2,1,0:T(8,128)(2,1)}, bf16[27,128,2048]{2,1,0:T(8,128)(2,1)S(1)}, u32[]{:S(2)}) %copy-start) | copy-done | bytes 14155800 | tf_op jit(solution)/shard_map/while
  299.6 8.5 %fusion.147 = f32[32,2048]{1,0:T(8,128)} fusion(bf16[27,128,2048]{2,1,0:T(8,128)(2,1)} %copy-done, f32[32,2048]{1,0:T(8,128)} %get-tuple-element.284, bf16[32,27,1024]{2,0,1:T(8,128)(2,1)} %get-tuple-element.296, s32[]{:T(128)S(6)} %select_n.2038, pred[]{:T(512)S(6)} %compare.180), kind=kOutput, calls=%fused_computation.1.clone.1 | convolution fusion | flops 453115904 | bytes 14901253 | tf_op jit(solution)/shard_map/while/body/eval_jaxpr/dot_general | solution.py:92
  308.1 0.8 copy-done.1
  308.9 4.3 %fusion.148 = f32[27,128,32]{1,2,0:T(8,128)S(1)} fusion(bf16[27,128,2048]{2,1,0:T(8,128)(2,1)S(1)} %copy-done.1, bf16[32,2048]{1,0:T(8,128)(2,1)S(1)} %copy-done.3), kind=kOutput, calls=%fused_computation.68.clone.1 | convolution fusion | flops 452984832 | bytes 14729216 | tf_op jit(solution)/shard_map/while/body/eval_jaxpr/dot_general | solution.py:93
  313.3 1.6 constant_dynamic-slice_fusion.2
  321.6 5.0 %copy-done = bf16[27,128,2048]{2,1,0:T(8,128)(2,1)} copy-done((bf16[27,128,2048]{2,1,0:T(8,128)(2,1)}, bf16[27,128,2048]{2,1,0:T(8,128)(2,1)S(1)}, u32[]{:S(2)}) %copy-start) | copy-done | bytes 14155800 | tf_op jit(solution)/shard_map/while
  326.6 8.5 %fusion.147 = f32[32,2048]{1,0:T(8,128)} fusion(bf16[27,128,2048]{2,1,0:T(8,128)(2,1)} %copy-done, f32[32,2048]{1,0:T(8,128)} %get-tuple-element.284, bf16[32,27,1024]{2,0,1:T(8,128)(2,1)} %get-tuple-element.296, s32[]{:T(128)S(6)} %select_n.2038, pred[]{:T(512)S(6)} %compare.180), kind=kOutput, calls=%fused_computation.1.clone.1 | convolution fusion | flops 453115904 | bytes 14901253 | tf_op jit(solution)/shard_map/while/body/eval_jaxpr/dot_general | solution.py:92
  335.2 0.8 copy-done.1
  336.0 4.3 %fusion.148 = f32[27,128,32]{1,2,0:T(8,128)S(1)} fusion(bf16[27,128,2048]{2,1,0:T(8,128)(2,1)S(1)} %copy-done.1, bf16[32,2048]{1,0:T(8,128)(2,1)S(1)} %copy-done.3), kind=kOutput, calls=%fused_computation.68.clone.1 | convolution fusion | flops 452984832 | bytes 14729216 | tf_op jit(solution)/shard_map/while/body/eval_jaxpr/dot_general | solution.py:93
  340.4 1.7 copy-done.2
  342.2 1.2 copy.9
  343.4 0.9 copy.7
  344.3 1.0 convert_element_type.16
  345.2 0.7 reshape.228
  346.0 44.9 %reduce-scatter.5.cloned.1.call-done = f32[32,27,128]{2,0,1:T(8,128)} async-done(((f32[32,27,1024]{2,0,1:T(8,128)}), f32[32,27,128]{2,0,1:T(8,128)}) %reduce-scatter.5.cloned.1.call-update) | async-done | bytes 442384 | tf_op jit(solution)/shard_map/reduce_scatter | solution.py:105
  390.8 1.8 broadcast_multiply_fusion
  (386 shorter events, 55.6 us)
Async XLA Ops:
  7.2 49.3 %all-gather.3.cloned.1.call-start = ((), (), s32[]{:S(2)}) async-start(), calls=%async_computation.2 | async-start | bytes 1990656 | tf_op jit(solution)/shard_map/all_gather | solution.py:69
  7.9 112.7 %all-gather.5.cloned.1.call-start = ((), (), s32[]{:S(2)}) async-start(), calls=%async_computation.3 | async-start | bytes 8650752 | tf_op jit(solution)/shard_map/all_gather | solution.py:79
  9.2 6.7 %collective-permute-start.1 = (bf16[32,1,1024]{2,1,0:T(2,128)(2,1)S(1)}, bf16[32,1,1024]{2,1,0:T(2,128)(2,1)S(1)}, u32[]{:S(2)}, u32[]{:S(2)}) collective-permute-start(bf16[32,1,1024]{2,1,0:T(2,128)(2,1)S(1)} %get-tuple-element.235), channel_id=1, source_target_pairs={{32,0},{64,32},{96,64},{128,96},{160,128},{192,160},{224,192},{33,... | collective-permute-start | bytes 196616 | tf_op jit(solution)/shard_map/ppermute | solution.py:20
  10.5 6.9 %collective-permute-start = (bf16[32,1,1024]{2,1,0:T(2,128)(2,1)S(1)}, bf16[32,1,1024]{2,1,0:T(2,128)(2,1)S(1)}, u32[]{:S(2)}, u32[]{:S(2)}) collective-permute-start(bf16[32,1,1024]{2,1,0:T(2,128)(2,1)S(1)} %get-tuple-element.234), channel_id=1, source_target_pairs={{0,32},{32,64},{64,96},{96,128},{128,160},{160,192},{192,224},{1,3... | collective-permute-start | bytes 196616 | tf_op jit(solution)/shard_map/ppermute | solution.py:17
  19.5 322.7 %reduce-scatter.7.cloned.1.call-start = ((), (), s32[]{:S(2)}) async-start(), calls=%async_computation.5 | async-start | bytes 8650752
  20.8 7.5 %collective-permute-start.3 = (bf16[32,1,1024]{2,1,0:T(2,128)(2,1)S(1)}, bf16[32,1,1024]{2,1,0:T(2,128)(2,1)S(1)}, u32[]{:S(2)}, u32[]{:S(2)}) collective-permute-start(bf16[32,1,1024]{2,1,0:T(2,128)(2,1)S(1)} %get-tuple-element.233), channel_id=1, source_target_pairs={{32,0},{64,32},{96,64},{128,96},{160,128},{192,160},{224,192},{33,... | collective-permute-start | bytes 196616 | tf_op jit(solution)/shard_map/ppermute | solution.py:20
  22.1 6.4 %collective-permute-start.2 = (bf16[32,1,1024]{2,1,0:T(2,128)(2,1)S(1)}, bf16[32,1,1024]{2,1,0:T(2,128)(2,1)S(1)}, u32[]{:S(2)}, u32[]{:S(2)}) collective-permute-start(bf16[32,1,1024]{2,1,0:T(2,128)(2,1)S(1)} %get-tuple-element.232), channel_id=1, source_target_pairs={{0,32},{32,64},{64,96},{96,128},{128,160},{160,192},{192,224},{1,3... | collective-permute-start | bytes 196616 | tf_op jit(solution)/shard_map/ppermute | solution.py:17
  73.8 317.0 %reduce-scatter.5.cloned.1.call-start = ((), (), s32[]{:S(2)}) async-start(), calls=%async_computation.4 | async-start | bytes 3981312 | tf_op jit(solution)/shard_map/reduce_scatter | solution.py:105
  129.5 5.1 %copy-start = (bf16[27,128,2048]{2,1,0:T(8,128)(2,1)}, bf16[27,128,2048]{2,1,0:T(8,128)(2,1)S(1)}, u32[]{:S(2)}) copy-start(bf16[27,128,2048]{2,1,0:T(8,128)(2,1)S(1)} %bitcast_dynamic-update-slice_fusion.31) | copy-start | bytes 42467332 | tf_op jit(solution)/shard_map/while
  134.5 10.5 %copy-start.1 = (bf16[27,128,2048]{2,1,0:T(8,128)(2,1)S(1)}, bf16[27,128,2048]{2,1,0:T(8,128)(2,1)}, u32[]{:S(2)}) copy-start(bf16[27,128,2048]{2,1,0:T(8,128)(2,1)} %copy-done) | copy-start | bytes 42467332 | tf_op jit(solution)/shard_map/while
  134.5 10.5 %copy-start.3 = (bf16[32,2048]{1,0:T(8,128)(2,1)S(1)}, bf16[32,2048]{1,0:T(8,128)(2,1)}, u32[]{:S(2)}) copy-start(bf16[32,2048]{1,0:T(8,128)(2,1)} %get-tuple-element.298) | copy-start | bytes 393220 | tf_op jit(solution)/shard_map/while
  157.7 5.5 %copy-start = (bf16[27,128,2048]{2,1,0:T(8,128)(2,1)}, bf16[27,128,2048]{2,1,0:T(8,128)(2,1)S(1)}, u32[]{:S(2)}) copy-start(bf16[27,128,2048]{2,1,0:T(8,128)(2,1)S(1)} %bitcast_dynamic-update-slice_fusion.31) | copy-start | bytes 42467332 | tf_op jit(solution)/shard_map/while
  163.2 9.6 %copy-start.1 = (bf16[27,128,2048]{2,1,0:T(8,128)(2,1)S(1)}, bf16[27,128,2048]{2,1,0:T(8,128)(2,1)}, u32[]{:S(2)}) copy-start(bf16[27,128,2048]{2,1,0:T(8,128)(2,1)} %copy-done) | copy-start | bytes 42467332 | tf_op jit(solution)/shard_map/while
  163.2 9.6 %copy-start.3 = (bf16[32,2048]{1,0:T(8,128)(2,1)S(1)}, bf16[32,2048]{1,0:T(8,128)(2,1)}, u32[]{:S(2)}) copy-start(bf16[32,2048]{1,0:T(8,128)(2,1)} %get-tuple-element.298) | copy-start | bytes 393220 | tf_op jit(solution)/shard_map/while
  185.5 5.1 %copy-start = (bf16[27,128,2048]{2,1,0:T(8,128)(2,1)}, bf16[27,128,2048]{2,1,0:T(8,128)(2,1)S(1)}, u32[]{:S(2)}) copy-start(bf16[27,128,2048]{2,1,0:T(8,128)(2,1)S(1)} %bitcast_dynamic-update-slice_fusion.31) | copy-start | bytes 42467332 | tf_op jit(solution)/shard_map/while
  190.6 9.8 %copy-start.1 = (bf16[27,128,2048]{2,1,0:T(8,128)(2,1)S(1)}, bf16[27,128,2048]{2,1,0:T(8,128)(2,1)}, u32[]{:S(2)}) copy-start(bf16[27,128,2048]{2,1,0:T(8,128)(2,1)} %copy-done) | copy-start | bytes 42467332 | tf_op jit(solution)/shard_map/while
  190.7 9.8 %copy-start.3 = (bf16[32,2048]{1,0:T(8,128)(2,1)S(1)}, bf16[32,2048]{1,0:T(8,128)(2,1)}, u32[]{:S(2)}) copy-start(bf16[32,2048]{1,0:T(8,128)(2,1)} %get-tuple-element.298) | copy-start | bytes 393220 | tf_op jit(solution)/shard_map/while
  213.2 5.1 %copy-start = (bf16[27,128,2048]{2,1,0:T(8,128)(2,1)}, bf16[27,128,2048]{2,1,0:T(8,128)(2,1)S(1)}, u32[]{:S(2)}) copy-start(bf16[27,128,2048]{2,1,0:T(8,128)(2,1)S(1)} %bitcast_dynamic-update-slice_fusion.31) | copy-start | bytes 42467332 | tf_op jit(solution)/shard_map/while
  218.2 9.5 %copy-start.1 = (bf16[27,128,2048]{2,1,0:T(8,128)(2,1)S(1)}, bf16[27,128,2048]{2,1,0:T(8,128)(2,1)}, u32[]{:S(2)}) copy-start(bf16[27,128,2048]{2,1,0:T(8,128)(2,1)} %copy-done) | copy-start | bytes 42467332 | tf_op jit(solution)/shard_map/while
  218.2 9.5 %copy-start.3 = (bf16[32,2048]{1,0:T(8,128)(2,1)S(1)}, bf16[32,2048]{1,0:T(8,128)(2,1)}, u32[]{:S(2)}) copy-start(bf16[32,2048]{1,0:T(8,128)(2,1)} %get-tuple-element.298) | copy-start | bytes 393220 | tf_op jit(solution)/shard_map/while
  240.4 5.1 %copy-start = (bf16[27,128,2048]{2,1,0:T(8,128)(2,1)}, bf16[27,128,2048]{2,1,0:T(8,128)(2,1)S(1)}, u32[]{:S(2)}) copy-start(bf16[27,128,2048]{2,1,0:T(8,128)(2,1)S(1)} %bitcast_dynamic-update-slice_fusion.31) | copy-start | bytes 42467332 | tf_op jit(solution)/shard_map/while
  245.5 9.3 %copy-start.1 = (bf16[27,128,2048]{2,1,0:T(8,128)(2,1)S(1)}, bf16[27,128,2048]{2,1,0:T(8,128)(2,1)}, u32[]{:S(2)}) copy-start(bf16[27,128,2048]{2,1,0:T(8,128)(2,1)} %copy-done) | copy-start | bytes 42467332 | tf_op jit(solution)/shard_map/while
  245.5 9.3 %copy-start.3 = (bf16[32,2048]{1,0:T(8,128)(2,1)S(1)}, bf16[32,2048]{1,0:T(8,128)(2,1)}, u32[]{:S(2)}) copy-start(bf16[32,2048]{1,0:T(8,128)(2,1)} %get-tuple-element.298) | copy-start | bytes 393220 | tf_op jit(solution)/shard_map/while
  267.5 5.1 %copy-start = (bf16[27,128,2048]{2,1,0:T(8,128)(2,1)}, bf16[27,128,2048]{2,1,0:T(8,128)(2,1)S(1)}, u32[]{:S(2)}) copy-start(bf16[27,128,2048]{2,1,0:T(8,128)(2,1)S(1)} %bitcast_dynamic-update-slice_fusion.31) | copy-start | bytes 42467332 | tf_op jit(solution)/shard_map/while
  272.5 9.3 %copy-start.1 = (bf16[27,128,2048]{2,1,0:T(8,128)(2,1)S(1)}, bf16[27,128,2048]{2,1,0:T(8,128)(2,1)}, u32[]{:S(2)}) copy-start(bf16[27,128,2048]{2,1,0:T(8,128)(2,1)} %copy-done) | copy-start | bytes 42467332 | tf_op jit(solution)/shard_map/while
  272.5 9.3 %copy-start.3 = (bf16[32,2048]{1,0:T(8,128)(2,1)S(1)}, bf16[32,2048]{1,0:T(8,128)(2,1)}, u32[]{:S(2)}) copy-start(bf16[32,2048]{1,0:T(8,128)(2,1)} %get-tuple-element.298) | copy-start | bytes 393220 | tf_op jit(solution)/shard_map/while
  294.5 5.1 %copy-start = (bf16[27,128,2048]{2,1,0:T(8,128)(2,1)}, bf16[27,128,2048]{2,1,0:T(8,128)(2,1)S(1)}, u32[]{:S(2)}) copy-start(bf16[27,128,2048]{2,1,0:T(8,128)(2,1)S(1)} %bitcast_dynamic-update-slice_fusion.31) | copy-start | bytes 42467332 | tf_op jit(solution)/shard_map/while
  299.6 9.3 %copy-start.1 = (bf16[27,128,2048]{2,1,0:T(8,128)(2,1)S(1)}, bf16[27,128,2048]{2,1,0:T(8,128)(2,1)}, u32[]{:S(2)}) copy-start(bf16[27,128,2048]{2,1,0:T(8,128)(2,1)} %copy-done) | copy-start | bytes 42467332 | tf_op jit(solution)/shard_map/while
  299.6 9.3 %copy-start.3 = (bf16[32,2048]{1,0:T(8,128)(2,1)S(1)}, bf16[32,2048]{1,0:T(8,128)(2,1)}, u32[]{:S(2)}) copy-start(bf16[32,2048]{1,0:T(8,128)(2,1)} %get-tuple-element.298) | copy-start | bytes 393220 | tf_op jit(solution)/shard_map/while
  321.6 5.1 %copy-start = (bf16[27,128,2048]{2,1,0:T(8,128)(2,1)}, bf16[27,128,2048]{2,1,0:T(8,128)(2,1)S(1)}, u32[]{:S(2)}) copy-start(bf16[27,128,2048]{2,1,0:T(8,128)(2,1)S(1)} %bitcast_dynamic-update-slice_fusion.31) | copy-start | bytes 42467332 | tf_op jit(solution)/shard_map/while
  326.6 9.3 %copy-start.1 = (bf16[27,128,2048]{2,1,0:T(8,128)(2,1)S(1)}, bf16[27,128,2048]{2,1,0:T(8,128)(2,1)}, u32[]{:S(2)}) copy-start(bf16[27,128,2048]{2,1,0:T(8,128)(2,1)} %copy-done) | copy-start | bytes 42467332 | tf_op jit(solution)/shard_map/while
  326.6 9.3 %copy-start.3 = (bf16[32,2048]{1,0:T(8,128)(2,1)S(1)}, bf16[32,2048]{1,0:T(8,128)(2,1)}, u32[]{:S(2)}) copy-start(bf16[32,2048]{1,0:T(8,128)(2,1)} %get-tuple-element.298) | copy-start | bytes 393220 | tf_op jit(solution)/shard_map/while
  340.4 1.8 copy-start.2
Sparse Core Ops, SparseCore 0:
  9.7 46.7 all-gather.2
  59.0 61.5 all-gather.4
  124.6 97.8 reduce-scatter.6
  342.3 48.5 reduce-scatter.4
where the time goes:
time: 400 us; the launch traced here: 399 us
  waiting for transfers between devices  118 us (30%)
  matrix products  112 us (28%)
  local copies, waits for them, and re-layouts  82.8 us (21%)
  other arithmetic  57.2 us (14%)
  between operations  14.1 us (4%)
  starting transfers between devices  12.2 us (3%)
    dot_general x8, matrix products, one_block(): jnp.dot(flat_weight, columns, preferred_element_type=jnp.float32)  69.5 us
    while x56, local copies, waits for them, and re-layouts  51.2 us
    all_gather x1, waiting for transfers between devices, on_device(): shard_rows = lax.all_gather(input_rim, 'col', axis=0, tiled=True)  46.7 us
    while x208, other arithmetic  45.3 us
    reduce_scatter x1, waiting for transfers between devices, on_device(): lax.psum_scatter(weight_sum, 'row', scatter_dimension=2, tiled=True) * scale  44.9 us
    dot_general x8, matrix products, one_block(): lax.dot_general(columns, grad_rows, (((1,), (1,)), ((), ())), preferred_e...  34.4 us
    all_gather x1, waiting for transfers between devices, on_device(): gathered_weight = lax.all_gather(weight, 'row', axis=2, tiled=True)  23.8 us
    unnamed x7, local copies, waits for them, and re-layouts  14.6 us
  transfers between devices with their start and end apart: 8, of which 6 were waited for; matrix products, arithmetic and copies ran while one was open for 50% of the time, Pallas kernels for 0%

commit v1 on v0

--- a/solution.py
+++ b/solution.py
@@ -7,6 +7,11 @@
 BX = 32
 BY = 32
 kernel_offsets = [(a, b, e) for a in (-1, 0, 1) for b in (-1, 0, 1) for e in (-1, 0, 1)]
+
+
+def all_by_exchange(block, mesh_axis, dim):
+    sent = jnp.stack([block] * lax.axis_size(mesh_axis))
+    return jnp.concatenate(lax.all_to_all(sent, mesh_axis, 0, 0), axis=dim)
 
 
 def extended(block, sides, width):
@@ -66,7 +71,7 @@
     width_dev = inputs.shape[0]
     planes = inputs.shape[1]
     extent = planes * BY * BX
-    gathered_weight = lax.all_gather(weight, "row", axis=2, tiled=True)
+    gathered_weight = all_by_exchange(weight, "row", 2)
     out_width = gathered_weight.shape[0]
     channels = gathered_weight.shape[2]
     input_rim = extended(inputs, (("row", 1),), 1)

time: 400 us -> 338 us (0.84)
  waiting for transfers between devices: 118 us -> 78.6 us
  local copies, waits for them, and re-layouts: 82.8 us -> 55.3 us
  starting transfers between devices: 12.2 us -> 19.6 us
    all_gather x1, waiting for transfers between devices: 46.7 us -> 0.01 us  [on_device(): shard_rows = lax.all_gather(input_rim, 'col', axis=0, tiled=True)]
    while x56 -> x40, local copies, waits for them, and re-layouts: 51.2 us -> 9.78 us
    all_to_all x0 -> x1, waiting for transfers between devices: none -> 29.1 us  [all_by_exchange(): return jnp.concatenate(lax.all_to_all(sent, mesh_axis, 0, 0), axis=dim)]
    all_gather x1 -> x0, waiting for transfers between devices: 23.8 us -> none  [on_device(): gathered_weight = lax.all_gather(weight, 'row', axis=2, tiled=True)]
    all_to_all x0 -> x1, starting transfers between devices: none -> 8.8 us  [all_by_exchange(): return jnp.concatenate(lax.all_to_all(sent, mesh_axis, 0, 0), axis=dim)]
    reshape x0 -> x3, local copies, waits for them, and re-layouts: none -> 7.14 us  [the longest x1 4.98 us: backward_columns(): return stacked.reshape(padded.shape[0] * 27, stacked.shape[2])]
    another operation x0 -> x2, local copies, waits for them, and re-layouts: none -> 6.43 us  [the longest x1 3.96 us: backward_columns(): stacked = jnp.stack(windows, axis=1)]
    unnamed x7 -> x11, local copies, waits for them, and re-layouts: 14.6 us -> 15.2 us
  transfers between devices with their start and end apart: 8 -> 8, of which waited for: 6 -> 4; matrix products, arithmetic and copies ran while one was open for 50% -> 61% of each run, Pallas kernels for 0% -> 0%
where the time goes in v1:
time: 338 us; the launch traced here: 337 us
  matrix products  110 us (33%)
  waiting for transfers between devices  78.6 us (23%)
  other arithmetic  56.3 us (17%)
  local copies, waits for them, and re-layouts  55.3 us (16%)
  starting transfers between devices  19.6 us (6%)
  between operations  14.1 us (4%)
    dot_general x8, matrix products, one_block(): jnp.dot(flat_weight, columns, preferred_element_type=jnp.float32)  68.8 us
    while x208, other arithmetic  45.3 us
    reduce_scatter x1, waiting for transfers between devices, on_device(): lax.psum_scatter(weight_sum, 'row', scatter_dimension=2, tiled=True) * scale  44.4 us
    dot_general x8, matrix products, one_block(): lax.dot_general(columns, grad_rows, (((1,), (1,)), ((), ())), preferred_e...  34.4 us
    all_to_all x1, waiting for transfers between devices, all_by_exchange(): return jnp.concatenate(lax.all_to_all(sent, mesh_axis, 0, 0), axis=dim)  29.1 us
    unnamed x11, local copies, waits for them, and re-layouts  15.2 us
    dynamic_slice x8, local copies, waits for them, and re-layouts, one_block(): lax.dynamic_slice_in_dim(shard_rows, b * block_rows, block_rows, 0)  12.8 us
    while x40, local copies, waits for them, and re-layouts  9.78 us
  transfers between devices with their start and end apart: 8, of which 4 were waited for; matrix products, arithmetic and copies ran while one was open for 61% of the time, Pallas kernels for 0%

profile of v1, /device:TPU:1, one launch (start us, length us, event | category | flops | bytes accessed | tf_op | source)
XLA Modules:
  0.0 336.6 jit_solution(5487486552122086934)
XLA Ops:
  7.2 1.2 fusion.96
  8.4 4.5 %collective-permute-start = (bf16[32,1,1024]{2,1,0:T(2,128)(2,1)S(1)}, bf16[32,1,1024]{2,1,0:T(2,128)(2,1)S(1)}, u32[]{:S(2)}, u32[]{:S(2)}) collective-permute-start(bf16[32,1,1024]{2,1,0:T(2,128)(2,1)S(1)} %get-tuple-element.246), channel_id=1, source_target_pairs={{0,32},{32,64},{64,96},{96,128},{128,160},{160,192},{192,224},{1,3... | collective-permute-start | bytes 196616 | tf_op jit(solution)/shard_map/ppermute | solution.py:22
  12.9 1.3 collective-permute-start.1
  14.2 0.8 collective-permute-done
  15.1 4.2 %collective-permute-done.1 = bf16[32,1,1024]{2,1,0:T(2,128)(2,1)S(1)} collective-permute-done((bf16[32,1,1024]{2,1,0:T(2,128)(2,1)S(1)}, bf16[32,1,1024]{2,1,0:T(2,128)(2,1)S(1)}, u32[]{:S(2)}, u32[]{:S(2)}) %collective-permute-start.1) | collective-permute-done | bytes 65568 | tf_op jit(solution)/shard_map/ppermute | solution.py:25
  19.3 2.1 pad_maximum_fusion
  21.4 1.2 fusion.95
  22.6 3.6 %collective-permute-start.2 = (bf16[32,1,1024]{2,1,0:T(2,128)(2,1)S(1)}, bf16[32,1,1024]{2,1,0:T(2,128)(2,1)S(1)}, u32[]{:S(2)}, u32[]{:S(2)}) collective-permute-start(bf16[32,1,1024]{2,1,0:T(2,128)(2,1)S(1)} %get-tuple-element.244), channel_id=1, source_target_pairs={{0,32},{32,64},{64,96},{96,128},{128,160},{160,192},{192,224},{1,3... | collective-permute-start | bytes 196616 | tf_op jit(solution)/shard_map/ppermute | solution.py:22
  26.1 1.3 collective-permute-start.3
  27.4 2.5 stack.403
  29.9 8.8 %all-to-all-start = ((bf16[8,32,27,128]{3,1,2,0:T(8,128)(2,1)}), bf16[8,32,27,128]{3,1,2,0:T(8,128)(2,1)S(1)}, u32[]{:S(2)}, u32[]{:S(2)}) async-start(bf16[8,32,27,128]{3,1,2,0:T(8,128)(2,1)} %stack.403), calls=%async_computation | async-start | bytes 3538944 | tf_op jit(solution)/shard_map/all_to_all | solution.py:14
  38.8 0.7 copy.57
  39.7 0.4 pad_maximum_fusion.1
  43.0 4.0 %copy.50 = bf16[32,27,2048]{2,1,0:T(8,128)(2,1)} copy(bf16[32,27,2048]{2,0,1:T(8,128)(2,1)S(1)} %bitcast_dynamic-update-slice_fusion.8) | data formatting | bytes 7077888 | tf_op jit(solution)/shard_map/stack | solution.py:57
  47.0 5.0 %reshape.241 = bf16[864,2048]{1,0:T(8,128)(2,1)} reshape(bf16[32,27,2048]{2,1,0:T(8,128)(2,1)} %copy.50) | data formatting | bytes 7077888 | tf_op jit(solution)/shard_map/reshape | solution.py:58
  51.9 29.1 %all-to-all-done = bf16[8,32,27,128]{3,1,2,0:T(8,128)(2,1)S(1)} async-done(((bf16[8,32,27,128]{3,1,2,0:T(8,128)(2,1)}), bf16[8,32,27,128]{3,1,2,0:T(8,128)(2,1)S(1)}, u32[]{:S(2)}, u32[]{:S(2)}) %all-to-all-start) | async-done | bytes 1769504 | tf_op jit(solution)/shard_map/all_to_all | solution.py:14
  81.0 0.7 copy.51
  81.7 1.4 copy-done.3
  83.1 7.0 %convolution_bitcast_fusion.1 = f32[1024,2048]{0,1:T(8,128)} fusion(bf16[864,2048]{1,0:T(8,128)(2,1)S(1)} %copy-done.3, bf16[108,8,8,128]{3,2,1,0:T(8,128)(2,1)S(1)} %bitcast.350), kind=kOutput, calls=%fused_computation.105 | convolution fusion | flops 3623878656 | bytes 13697024 | tf_op jit(solution)/shard_map/dot_general | solution.py:114
  90.1 9.2 %copy.53 = f32[1024,2048]{1,0:T(8,128)} copy(f32[1024,2048]{0,1:T(8,128)} %convolution_bitcast_fusion.1) | data formatting | bytes 16777216
  99.3 1.5 copy_bitcast_fusion
  100.8 0.4 broadcast_in_dim.490
  101.3 177.0 %while.19 = (s32[]{:T(128)}, f32[32,2048]{1,0:T(8,128)}, f32[1024,864]{0,1:T(8,128)S(1)}, bf16[32,27,1024]{2,0,1:T(8,128)(2,1)}, bf16[1024,4,1024]{2,1,0:T(4,128...) while((s32[]{:T(128)}, f32[32,2048]{1,0:T(8,128)}, ...), condition=%wide.region_1.2_spmd.clone, body=%wide.region_0.1_spmd.clone.sunk | while | flops 913793024 | bytes 124436712 | solution.py:106
  101.5 1.6 constant_dynamic-slice_fusion.2
  109.7 4.3 %fusion.150 = f32[27,128,32]{1,2,0:T(8,128)S(1)} fusion(bf16[27,128,2048]{2,1,0:T(8,128)(2,1)S(1)} %bitcast_dynamic-update-slice_fusion.31, bf16[32,2048]{1,0:T(8,128)(2,1)S(1)} %copy-done.2), kind=kOutput, calls=%fused_computation.68.clone.1 | convolution fusion | flops 452984832 | bytes 14729216 | tf_op jit(solution)/shard_map/while/body/eval_jaxpr/dot_general | solution.py:98
  114.1 1.2 copy-done
  115.3 9.1 %fusion.149 = f32[32,2048]{1,0:T(8,128)} fusion(bf16[27,128,2048]{2,1,0:T(8,128)(2,1)} %copy-done, f32[32,2048]{1,0:T(8,128)} %get-tuple-element.296, bf16[32,27,1024]{2,0,1:T(8,128)(2,1)} %get-tuple-element.308, s32[]{:T(128)S(6)} %select_n.2038, pred[]{:T(512)S(6)} %compare.180), kind=kOutput, calls=%fused_computation.1.clone.1 | convolution fusion | flops 453115904 | bytes 14901253 | tf_op jit(solution)/shard_map/while/body/eval_jaxpr/dot_general | solution.py:97
  124.4 1.6 constant_dynamic-slice_fusion.2
  126.1 0.4 copy.66
  132.8 4.3 %fusion.150 = f32[27,128,32]{1,2,0:T(8,128)S(1)} fusion(bf16[27,128,2048]{2,1,0:T(8,128)(2,1)S(1)} %bitcast_dynamic-update-slice_fusion.31, bf16[32,2048]{1,0:T(8,128)(2,1)S(1)} %copy-done.2), kind=kOutput, calls=%fused_computation.68.clone.1 | convolution fusion | flops 452984832 | bytes 14729216 | tf_op jit(solution)/shard_map/while/body/eval_jaxpr/dot_general | solution.py:98
  137.1 1.2 copy-done
  138.3 8.6 %fusion.149 = f32[32,2048]{1,0:T(8,128)} fusion(bf16[27,128,2048]{2,1,0:T(8,128)(2,1)} %copy-done, f32[32,2048]{1,0:T(8,128)} %get-tuple-element.296, bf16[32,27,1024]{2,0,1:T(8,128)(2,1)} %get-tuple-element.308, s32[]{:T(128)S(6)} %select_n.2038, pred[]{:T(512)S(6)} %compare.180), kind=kOutput, calls=%fused_computation.1.clone.1 | convolution fusion | flops 453115904 | bytes 14901253 | tf_op jit(solution)/shard_map/while/body/eval_jaxpr/dot_general | solution.py:97
  146.9 1.6 constant_dynamic-slice_fusion.2
  148.5 0.4 copy.66
  155.2 4.3 %fusion.150 = f32[27,128,32]{1,2,0:T(8,128)S(1)} fusion(bf16[27,128,2048]{2,1,0:T(8,128)(2,1)S(1)} %bitcast_dynamic-update-slice_fusion.31, bf16[32,2048]{1,0:T(8,128)(2,1)S(1)} %copy-done.2), kind=kOutput, calls=%fused_computation.68.clone.1 | convolution fusion | flops 452984832 | bytes 14729216 | tf_op jit(solution)/shard_map/while/body/eval_jaxpr/dot_general | solution.py:98
  159.5 0.7 copy-done
  160.3 8.8 %fusion.149 = f32[32,2048]{1,0:T(8,128)} fusion(bf16[27,128,2048]{2,1,0:T(8,128)(2,1)} %copy-done, f32[32,2048]{1,0:T(8,128)} %get-tuple-element.296, bf16[32,27,1024]{2,0,1:T(8,128)(2,1)} %get-tuple-element.308, s32[]{:T(128)S(6)} %select_n.2038, pred[]{:T(512)S(6)} %compare.180), kind=kOutput, calls=%fused_computation.1.clone.1 | convolution fusion | flops 453115904 | bytes 14901253 | tf_op jit(solution)/shard_map/while/body/eval_jaxpr/dot_general | solution.py:97
  169.0 1.6 constant_dynamic-slice_fusion.2
  177.4 4.3 %fusion.150 = f32[27,128,32]{1,2,0:T(8,128)S(1)} fusion(bf16[27,128,2048]{2,1,0:T(8,128)(2,1)S(1)} %bitcast_dynamic-update-slice_fusion.31, bf16[32,2048]{1,0:T(8,128)(2,1)S(1)} %copy-done.2), kind=kOutput, calls=%fused_computation.68.clone.1 | convolution fusion | flops 452984832 | bytes 14729216 | tf_op jit(solution)/shard_map/while/body/eval_jaxpr/dot_general | solution.py:98
  181.7 0.7 copy-done
  182.5 8.6 %fusion.149 = f32[32,2048]{1,0:T(8,128)} fusion(bf16[27,128,2048]{2,1,0:T(8,128)(2,1)} %copy-done, f32[32,2048]{1,0:T(8,128)} %get-tuple-element.296, bf16[32,27,1024]{2,0,1:T(8,128)(2,1)} %get-tuple-element.308, s32[]{:T(128)S(6)} %select_n.2038, pred[]{:T(512)S(6)} %compare.180), kind=kOutput, calls=%fused_computation.1.clone.1 | convolution fusion | flops 453115904 | bytes 14901253 | tf_op jit(solution)/shard_map/while/body/eval_jaxpr/dot_general | solution.py:97
  191.1 1.6 constant_dynamic-slice_fusion.2
  199.4 4.3 %fusion.150 = f32[27,128,32]{1,2,0:T(8,128)S(1)} fusion(bf16[27,128,2048]{2,1,0:T(8,128)(2,1)S(1)} %bitcast_dynamic-update-slice_fusion.31, bf16[32,2048]{1,0:T(8,128)(2,1)S(1)} %copy-done.2), kind=kOutput, calls=%fused_computation.68.clone.1 | convolution fusion | flops 452984832 | bytes 14729216 | tf_op jit(solution)/shard_map/while/body/eval_jaxpr/dot_general | solution.py:98
  203.7 0.7 copy-done
  204.5 8.4 %fusion.149 = f32[32,2048]{1,0:T(8,128)} fusion(bf16[27,128,2048]{2,1,0:T(8,128)(2,1)} %copy-done, f32[32,2048]{1,0:T(8,128)} %get-tuple-element.296, bf16[32,27,1024]{2,0,1:T(8,128)(2,1)} %get-tuple-element.308, s32[]{:T(128)S(6)} %select_n.2038, pred[]{:T(512)S(6)} %compare.180), kind=kOutput, calls=%fused_computation.1.clone.1 | convolution fusion | flops 453115904 | bytes 14901253 | tf_op jit(solution)/shard_map/while/body/eval_jaxpr/dot_general | solution.py:97
  212.9 1.6 constant_dynamic-slice_fusion.2
  221.2 4.3 %fusion.150 = f32[27,128,32]{1,2,0:T(8,128)S(1)} fusion(bf16[27,128,2048]{2,1,0:T(8,128)(2,1)S(1)} %bitcast_dynamic-update-slice_fusion.31, bf16[32,2048]{1,0:T(8,128)(2,1)S(1)} %copy-done.2), kind=kOutput, calls=%fused_computation.68.clone.1 | convolution fusion | flops 452984832 | bytes 14729216 | tf_op jit(solution)/shard_map/while/body/eval_jaxpr/dot_general | solution.py:98
  225.5 0.7 copy-done
  226.3 8.4 %fusion.149 = f32[32,2048]{1,0:T(8,128)} fusion(bf16[27,128,2048]{2,1,0:T(8,128)(2,1)} %copy-done, f32[32,2048]{1,0:T(8,128)} %get-tuple-element.296, bf16[32,27,1024]{2,0,1:T(8,128)(2,1)} %get-tuple-element.308, s32[]{:T(128)S(6)} %select_n.2038, pred[]{:T(512)S(6)} %compare.180), kind=kOutput, calls=%fused_computation.1.clone.1 | convolution fusion | flops 453115904 | bytes 14901253 | tf_op jit(solution)/shard_map/while/body/eval_jaxpr/dot_general | solution.py:97
  234.7 1.6 constant_dynamic-slice_fusion.2
  243.0 4.3 %fusion.150 = f32[27,128,32]{1,2,0:T(8,128)S(1)} fusion(bf16[27,128,2048]{2,1,0:T(8,128)(2,1)S(1)} %bitcast_dynamic-update-slice_fusion.31, bf16[32,2048]{1,0:T(8,128)(2,1)S(1)} %copy-done.2), kind=kOutput, calls=%fused_computation.68.clone.1 | convolution fusion | flops 452984832 | bytes 14729216 | tf_op jit(solution)/shard_map/while/body/eval_jaxpr/dot_general | solution.py:98
  247.3 0.7 copy-done
  248.1 8.4 %fusion.149 = f32[32,2048]{1,0:T(8,128)} fusion(bf16[27,128,2048]{2,1,0:T(8,128)(2,1)} %copy-done, f32[32,2048]{1,0:T(8,128)} %get-tuple-element.296, bf16[32,27,1024]{2,0,1:T(8,128)(2,1)} %get-tuple-element.308, s32[]{:T(128)S(6)} %select_n.2038, pred[]{:T(512)S(6)} %compare.180), kind=kOutput, calls=%fused_computation.1.clone.1 | convolution fusion | flops 453115904 | bytes 14901253 | tf_op jit(solution)/shard_map/while/body/eval_jaxpr/dot_general | solution.py:97
  256.5 1.6 constant_dynamic-slice_fusion.2
  264.8 4.3 %fusion.150 = f32[27,128,32]{1,2,0:T(8,128)S(1)} fusion(bf16[27,128,2048]{2,1,0:T(8,128)(2,1)S(1)} %bitcast_dynamic-update-slice_fusion.31, bf16[32,2048]{1,0:T(8,128)(2,1)S(1)} %copy-done.2), kind=kOutput, calls=%fused_computation.68.clone.1 | convolution fusion | flops 452984832 | bytes 14729216 | tf_op jit(solution)/shard_map/while/body/eval_jaxpr/dot_general | solution.py:98
  269.1 0.7 copy-done
  269.9 8.4 %fusion.149 = f32[32,2048]{1,0:T(8,128)} fusion(bf16[27,128,2048]{2,1,0:T(8,128)(2,1)} %copy-done, f32[32,2048]{1,0:T(8,128)} %get-tuple-element.296, bf16[32,27,1024]{2,0,1:T(8,128)(2,1)} %get-tuple-element.308, s32[]{:T(128)S(6)} %select_n.2038, pred[]{:T(512)S(6)} %compare.180), kind=kOutput, calls=%fused_computation.1.clone.1 | convolution fusion | flops 453115904 | bytes 14901253 | tf_op jit(solution)/shard_map/while/body/eval_jaxpr/dot_general | solution.py:97
  278.3 1.8 copy-done.1
  280.1 1.2 copy.54
  281.3 0.9 copy.52
  282.2 1.0 convert_element_type.16
  283.2 0.7 reshape.239
  283.9 44.4 %reduce-scatter.5.cloned.1.call-done = f32[32,27,128]{2,0,1:T(8,128)} async-done(((f32[32,27,1024]{2,0,1:T(8,128)}), f32[32,27,128]{2,0,1:T(8,128)}) %reduce-scatter.5.cloned.1.call-update) | async-done | bytes 442384 | tf_op jit(solution)/shard_map/reduce_scatter | solution.py:110
  328.3 1.8 broadcast_multiply_fusion
  (378 shorter events, 54.0 us)
Async XLA Ops:
  7.2 93.7 %all-gather.2.cloned.1.call-start = ((), (), s32[]{:S(2)}) async-start(), calls=%async_computation.3 | async-start | bytes 8650752 | tf_op jit(solution)/shard_map/all_gather | solution.py:84
  8.4 30.4 %copy-start.4 = (bf16[32,2,1024]{2,1,0:T(2,128)(2,1)S(1)}, bf16[32,2,1024]{2,1,0:T(2,128)(2,1)}, u32[]{:S(2)}) copy-start(bf16[32,2,1024]{2,1,0:T(2,128)(2,1)} %param.7) | copy-start | bytes 393220
  8.4 6.7 %collective-permute-start = (bf16[32,1,1024]{2,1,0:T(2,128)(2,1)S(1)}, bf16[32,1,1024]{2,1,0:T(2,128)(2,1)S(1)}, u32[]{:S(2)}, u32[]{:S(2)}) collective-permute-start(bf16[32,1,1024]{2,1,0:T(2,128)(2,1)S(1)} %get-tuple-element.246), channel_id=1, source_target_pairs={{0,32},{32,64},{64,96},{96,128},{128,160},{160,192},{192,224},{1,3... | collective-permute-start | bytes 196616 | tf_op jit(solution)/shard_map/ppermute | solution.py:22
  12.9 6.3 %collective-permute-start.1 = (bf16[32,1,1024]{2,1,0:T(2,128)(2,1)S(1)}, bf16[32,1,1024]{2,1,0:T(2,128)(2,1)S(1)}, u32[]{:S(2)}, u32[]{:S(2)}) collective-permute-start(bf16[32,1,1024]{2,1,0:T(2,128)(2,1)S(1)} %get-tuple-element.247), channel_id=1, source_target_pairs={{32,0},{64,32},{96,64},{128,96},{160,128},{192,160},{224,192},{33,... | collective-permute-start | bytes 196616 | tf_op jit(solution)/shard_map/ppermute | solution.py:25
  22.6 17.1 %collective-permute-start.2 = (bf16[32,1,1024]{2,1,0:T(2,128)(2,1)S(1)}, bf16[32,1,1024]{2,1,0:T(2,128)(2,1)S(1)}, u32[]{:S(2)}, u32[]{:S(2)}) collective-permute-start(bf16[32,1,1024]{2,1,0:T(2,128)(2,1)S(1)} %get-tuple-element.244), channel_id=1, source_target_pairs={{0,32},{32,64},{64,96},{96,128},{128,160},{160,192},{192,224},{1,3... | collective-permute-start | bytes 196616 | tf_op jit(solution)/shard_map/ppermute | solution.py:22
  26.1 13.5 %collective-permute-start.3 = (bf16[32,1,1024]{2,1,0:T(2,128)(2,1)S(1)}, bf16[32,1,1024]{2,1,0:T(2,128)(2,1)S(1)}, u32[]{:S(2)}, u32[]{:S(2)}) collective-permute-start(bf16[32,1,1024]{2,1,0:T(2,128)(2,1)S(1)} %get-tuple-element.245), channel_id=1, source_target_pairs={{32,0},{64,32},{96,64},{128,96},{160,128},{192,160},{224,192},{33,... | collective-permute-start | bytes 196616 | tf_op jit(solution)/shard_map/ppermute | solution.py:25
  29.9 51.1 %all-to-all-start = ((bf16[8,32,27,128]{3,1,2,0:T(8,128)(2,1)}), bf16[8,32,27,128]{3,1,2,0:T(8,128)(2,1)S(1)}, u32[]{:S(2)}, u32[]{:S(2)}) async-start(bf16[8,32,27,128]{3,1,2,0:T(8,128)(2,1)} %stack.403), calls=%async_computation | async-start | bytes 3538944 | tf_op jit(solution)/shard_map/all_to_all | solution.py:14
  38.7 241.4 %reduce-scatter.7.cloned.1.call-start = ((), (), s32[]{:S(2)}) async-start(), calls=%async_computation.5 | async-start | bytes 8650752
  81.0 2.1 copy-start.3
  99.3 229.0 %reduce-scatter.5.cloned.1.call-start = ((), (), s32[]{:S(2)}) async-start(), calls=%async_computation.4 | async-start | bytes 3981312 | tf_op jit(solution)/shard_map/reduce_scatter | solution.py:110
  108.6 1.1 copy-start.2
  109.7 5.5 %copy-start = (bf16[27,128,2048]{2,1,0:T(8,128)(2,1)}, bf16[27,128,2048]{2,1,0:T(8,128)(2,1)S(1)}, u32[]{:S(2)}) copy-start(bf16[27,128,2048]{2,1,0:T(8,128)(2,1)S(1)} %bitcast_dynamic-update-slice_fusion.31) | copy-start | bytes 42467332 | tf_op jit(solution)/shard_map/while
  131.6 1.1 copy-start.2
  132.7 5.5 %copy-start = (bf16[27,128,2048]{2,1,0:T(8,128)(2,1)}, bf16[27,128,2048]{2,1,0:T(8,128)(2,1)S(1)}, u32[]{:S(2)}) copy-start(bf16[27,128,2048]{2,1,0:T(8,128)(2,1)S(1)} %bitcast_dynamic-update-slice_fusion.31) | copy-start | bytes 42467332 | tf_op jit(solution)/shard_map/while
  154.1 1.1 copy-start.2
  155.2 5.1 %copy-start = (bf16[27,128,2048]{2,1,0:T(8,128)(2,1)}, bf16[27,128,2048]{2,1,0:T(8,128)(2,1)S(1)}, u32[]{:S(2)}) copy-start(bf16[27,128,2048]{2,1,0:T(8,128)(2,1)S(1)} %bitcast_dynamic-update-slice_fusion.31) | copy-start | bytes 42467332 | tf_op jit(solution)/shard_map/while
  176.3 1.1 copy-start.2
  177.3 5.1 %copy-start = (bf16[27,128,2048]{2,1,0:T(8,128)(2,1)}, bf16[27,128,2048]{2,1,0:T(8,128)(2,1)S(1)}, u32[]{:S(2)}) copy-start(bf16[27,128,2048]{2,1,0:T(8,128)(2,1)S(1)} %bitcast_dynamic-update-slice_fusion.31) | copy-start | bytes 42467332 | tf_op jit(solution)/shard_map/while
  198.3 1.1 copy-start.2
  199.4 5.1 %copy-start = (bf16[27,128,2048]{2,1,0:T(8,128)(2,1)}, bf16[27,128,2048]{2,1,0:T(8,128)(2,1)S(1)}, u32[]{:S(2)}) copy-start(bf16[27,128,2048]{2,1,0:T(8,128)(2,1)S(1)} %bitcast_dynamic-update-slice_fusion.31) | copy-start | bytes 42467332 | tf_op jit(solution)/shard_map/while
  220.1 1.1 copy-start.2
  221.2 5.1 %copy-start = (bf16[27,128,2048]{2,1,0:T(8,128)(2,1)}, bf16[27,128,2048]{2,1,0:T(8,128)(2,1)S(1)}, u32[]{:S(2)}) copy-start(bf16[27,128,2048]{2,1,0:T(8,128)(2,1)S(1)} %bitcast_dynamic-update-slice_fusion.31) | copy-start | bytes 42467332 | tf_op jit(solution)/shard_map/while
  241.9 1.1 copy-start.2
  243.0 5.1 %copy-start = (bf16[27,128,2048]{2,1,0:T(8,128)(2,1)}, bf16[27,128,2048]{2,1,0:T(8,128)(2,1)S(1)}, u32[]{:S(2)}) copy-start(bf16[27,128,2048]{2,1,0:T(8,128)(2,1)S(1)} %bitcast_dynamic-update-slice_fusion.31) | copy-start | bytes 42467332 | tf_op jit(solution)/shard_map/while
  263.7 1.1 copy-start.2
  264.8 5.1 %copy-start = (bf16[27,128,2048]{2,1,0:T(8,128)(2,1)}, bf16[27,128,2048]{2,1,0:T(8,128)(2,1)S(1)}, u32[]{:S(2)}) copy-start(bf16[27,128,2048]{2,1,0:T(8,128)(2,1)S(1)} %bitcast_dynamic-update-slice_fusion.31) | copy-start | bytes 42467332 | tf_op jit(solution)/shard_map/while
  278.3 1.8 copy-start.1
Sparse Core Ops, SparseCore 0:
  21.5 61.9 all-gather.1
  99.4 97.1 reduce-scatter.6
  280.2 48.0 reduce-scatter.4
